TPU v7x, 32 devices: a whole 2x2x4 slice. The times are simulated.
32 devices in a mesh: mem: 16 (over z, y, x), row: 2 (over core).
Axes of the slice: x: 2, y: 2, z: 4, core: 2. Of those that a mesh axis runs over, the one named last changes fastest.
Arguments:
- realization_stack: float32 [16, 5, 32, 256], P('mem', None, 'row'), may hold values from -6 to 6
- velocity: float32 [2, 32, 256], P(None, 'row'), may hold values from -0.25 to 0.25
- diffusion: float32 [5], replicated, may hold values from 0.04 to 0.12
- obs_cell: int32 [2048], replicated, may hold values from 0 to 40959
- obs_order: int32 [2048], replicated, may hold values from 0 to 2047, each once
- obs_value: float32 [2048], replicated, may hold values from -6 to 6
- obs_var: float32 [2048], replicated, may hold values from 0.2 to 2
- field_mask: int32 [5, 5], replicated, may hold values 0 or 1
Outputs:
- analysis: float32 [16, 5, 2, 16, 256], P(None, None, 'row', 'mem')
Inputs may be any that keep to these rules, and one draw needn't show every extreme that they name: `obs_cell`: a flat index field * 32 * 256 + row * 256 + column. `obs_order`: each of 0 to 2047 exactly once.
All inputs are finite; a program needn't handle non-finite values.
Results may differ from a plain program's by a relative error of at most 0.0003.
Values sent between devices are 32-bit elements; how exact they have to be, the bound alone decides.
No kernel may reach another device: no remote copies, remote signals or barrier semaphores. Data moves between devices by JAX's collectives and lax.ppermute only.
A program may use at most 64 MiB of HBM per device.

v0:
```python
import jax
import jax.numpy as jnp
from jax import lax
from jax.sharding import PartitionSpec as P

SUBSTEPS = 4
BATCHES = 2
LOC_HALF = 32
precise = lax.Precision.HIGHEST


def extended(shard, sides, width):
    for axis, dim in sides:
        count, length = (lax.axis_size(axis), shard.shape[dim])
        up = [(i, (i + 1) % count) for i in range(count - 1)]
        down = [(j, i) for i, j in up]
        last = lax.slice_in_dim(shard, length - width, length, axis=dim)
        initial = lax.slice_in_dim(shard, 0, width, axis=dim)
        before = lax.ppermute(last, axis, up)
        after = lax.ppermute(initial, axis, down)
        shard = jnp.concatenate([before, shard, after], axis=dim)
    return shard


def advance(padded, velocity, diffusion):
    spec_pad = ((0, 0),) * (padded.ndim - 1) + ((1, 1),)
    col_padded = jnp.pad(padded, spec_pad)
    centre = col_padded[..., 1:-1, 1:-1]
    north_cell = col_padded[..., :-2, 1:-1]
    south_cell = col_padded[..., 2:, 1:-1]
    west_cell = col_padded[..., 1:-1, :-2]
    east_cell = col_padded[..., 1:-1, 2:]
    along_col = velocity[0]
    along_row = velocity[1]
    spread = north_cell + south_cell + west_cell + east_cell - 4.0 * centre
    carried = (
        jnp.maximum(along_col, 0.0) * (centre - west_cell)
        + jnp.minimum(along_col, 0.0) * (east_cell - centre)
        + jnp.maximum(along_row, 0.0) * (centre - north_cell)
        + jnp.minimum(along_row, 0.0) * (south_cell - centre)
    )
    return centre + diffusion[:, None, None] * spread - carried


def gaspari(dist_sq):
    scaled = jnp.sqrt(dist_sq) / LOC_HALF
    clipped = jnp.maximum(scaled, 1.0)
    inner_part = (
        ((-0.25 * scaled + 0.5) * scaled + 0.625) * scaled - 5.0 / 3.0
    ) * scaled * scaled + 1.0
    outer_part = (
        ((((scaled / 12.0 - 0.5) * scaled + 0.625) * scaled + 5.0 / 3.0) * scaled - 5.0) * scaled
        + 4.0
        - 2.0 / (3.0 * clipped)
    )
    return jnp.where(scaled <= 1.0, inner_part, jnp.where(scaled <= 2.0, outer_part, 0.0))


def decode(flat_cells, total_rows, n_cols):
    field_ids = flat_cells // (total_rows * n_cols)
    row_ids = flat_cells // n_cols % total_rows
    col_ids = flat_cells % n_cols
    return (field_ids, row_ids, col_ids)


def innovations(priors, obs_values, obs_noise):
    members = priors.shape[0]
    average = jnp.mean(priors, axis=0)
    anomaly = priors - average
    spread = jnp.sum(anomaly * anomaly, axis=0) / (members - 1)
    variance_sum = spread + obs_noise
    root_sum = jnp.sqrt(variance_sum)
    shrink = 1.0 / (root_sum * (jnp.sqrt(obs_noise) + root_sum))
    adjust = (obs_values - average) / variance_sum - shrink * anomaly
    return (anomaly, adjust)


def regress(
    ensemble_now, base_row, obs_field, obs_row, obs_col, anomaly, adjust, field_mask, n_cols
):
    members, n_cells = ensemble_now.shape
    n_fields = field_mask.shape[0]
    per_field = n_cells // n_fields
    local_ids = lax.iota(jnp.int32, per_field)
    cell_row = (base_row + local_ids // n_cols).astype(jnp.float32)
    cell_col = (local_ids % n_cols).astype(jnp.float32)
    centred = ensemble_now - jnp.mean(ensemble_now, axis=0)
    mask_float = field_mask.astype(jnp.float32)
    total_obs = obs_field.shape[0]
    obs_block = min(256, total_obs)
    increment = jnp.zeros_like(ensemble_now)
    for offset in range(0, total_obs, obs_block):
        row_gap = cell_row[:, None] - obs_row[None, offset : offset + obs_block].astype(jnp.float32)
        col_gap = cell_col[:, None] - obs_col[None, offset : offset + obs_block].astype(jnp.float32)
        closeness = gaspari(row_gap * row_gap + col_gap * col_gap)
        field_hot = (
            obs_field[None, offset : offset + obs_block] == lax.iota(jnp.int32, n_fields)[:, None]
        ).astype(jnp.float32)
        allowed = jnp.dot(mask_float, field_hot, precision=precise)
        covariance = lax.dot_general(
            centred,
            anomaly[:, offset : offset + obs_block],
            (((0,), (0,)), ((), ())),
            precision=precise,
        )
        weights = (
            covariance.reshape(n_fields, per_field, obs_block)
            * (closeness[None] * allowed[:, None, :])
            / (members - 1)
        )
        increment = increment + lax.dot_general(
            adjust[:, offset : offset + obs_block],
            weights.reshape(n_cells, obs_block),
            (((1,), (1,)), ((), ())),
            precision=precise,
        )
    return ensemble_now + increment


def per_device(
    realization_stack, velocity, diffusion, obs_cell, obs_order, obs_value, obs_var, field_mask
):
    local_members = realization_stack.shape[0]
    n_fields = realization_stack.shape[1]
    rows_here = realization_stack.shape[2]
    n_cols = realization_stack.shape[3]
    n_mem = lax.axis_size("mem")
    n_slab = lax.axis_size("row")
    total_members = local_members * n_mem
    total_rows = rows_here * n_slab
    slab_index = lax.axis_index("row")
    member_index = lax.axis_index("mem")
    row_sub = rows_here // n_mem
    current = realization_stack
    for substep in range(SUBSTEPS):
        padded = extended(current, (("row", 2),), 1)
        current = advance(padded, velocity, diffusion)
    field_all, row_all, col_all = decode(obs_cell, total_rows, n_cols)
    batch_size = obs_cell.shape[0] // BATCHES
    layout = lax.all_to_all(current, "mem", split_axis=2, concat_axis=0, tiled=True)
    ensemble_now = layout.reshape(total_members, -1)
    base_row = slab_index * rows_here + member_index * row_sub
    for batch_num in range(BATCHES):
        picked = obs_order[batch_num * batch_size : (batch_num + 1) * batch_size]
        obs_field = field_all[picked]
        obs_row = row_all[picked]
        obs_col = col_all[picked]
        owned = ((obs_row >= base_row) & (obs_row < base_row + row_sub)).astype(jnp.float32)
        local_ids = (
            obs_field * row_sub * n_cols
            + jnp.clip(obs_row - base_row, 0, row_sub - 1) * n_cols
            + obs_col
        )
        partial_priors = jnp.take(ensemble_now, local_ids, axis=1) * owned[None, :]
        priors = lax.psum(partial_priors, ("mem", "row"))
        anomaly, adjust = innovations(priors, obs_value[picked], obs_var[picked])
        ensemble_now = regress(
            ensemble_now, base_row, obs_field, obs_row, obs_col, anomaly, adjust, field_mask, n_cols
        )
    return ensemble_now.reshape(total_members, n_fields, 1, row_sub, n_cols)


def solution(mesh):
    in_specs = (P("mem", None, "row", None), P(None, "row", None), P(), P(), P(), P(), P(), P())
    out_specs = P(None, None, "row", "mem", None)
    return jax.shard_map(
        per_device, mesh=mesh, in_specs=in_specs, out_specs=out_specs, check_vma=False
    )
```

profile of v0, /device:TPU:0, one launch (start us, length us, event | category | flops | bytes accessed | tf_op | source)
XLA Modules:
  0.0 403.0 jit_solution(6026265140585205028)
XLA Ops:
  6.5 1.0 copy.33
  7.5 1.3 collective-permute-start.1
  8.8 3.0 collective-permute-start
  13.3 6.1 %gather_fusion.8 = s32[1024]{0:T(1024)S(1)} fusion(s32[2048]{0:T(1024)S(1)} %get-tuple-element.33, s32[1024]{0:T(1024)S(1)} %get-tuple-element.28), kind=kCustom, calls=%fused_computation.10 | custom fusion | bytes 12288 | tf_op jit(solution)/shard_map/gather | solution.py:147
  19.4 6.2 %gather_fusion.7 = s32[1024]{0:T(1024)S(1)} fusion(s32[2048]{0:T(1024)S(1)} %get-tuple-element.32, s32[1024]{0:T(1024)S(1)} %get-tuple-element.28), kind=kCustom, calls=%fused_computation.9 | custom fusion | bytes 12288 | tf_op jit(solution)/shard_map/gather | solution.py:146
  25.6 6.2 %gather_fusion.3 = s32[1024]{0:T(1024)S(1)} fusion(s32[2048]{0:T(1024)S(1)} %get-tuple-element.33, s32[1024]{0:T(1024)S(1)} %get-tuple-element.29), kind=kCustom, calls=%fused_computation.5 | custom fusion | bytes 12288 | tf_op jit(solution)/shard_map/gather | solution.py:147
  31.8 6.2 %gather_fusion.2 = s32[1024]{0:T(1024)S(1)} fusion(s32[2048]{0:T(1024)S(1)} %get-tuple-element.32, s32[1024]{0:T(1024)S(1)} %get-tuple-element.29), kind=kCustom, calls=%fused_computation.4 | custom fusion | bytes 12288 | tf_op jit(solution)/shard_map/gather | solution.py:146
  37.9 6.2 %gather_fusion.1 = s32[1024]{0:T(1024)S(1)} fusion(s32[2048]{0:T(1024)S(1)} %get-tuple-element.34, s32[1024]{0:T(1024)S(1)} %get-tuple-element.29), kind=kCustom, calls=%fused_computation.3 | custom fusion | bytes 12288 | tf_op jit(solution)/shard_map/gather | solution.py:145
  44.1 6.2 %gather_fusion.6 = s32[1024]{0:T(1024)S(1)} fusion(s32[2048]{0:T(1024)S(1)} %get-tuple-element.34, s32[1024]{0:T(1024)S(1)} %get-tuple-element.28), kind=kCustom, calls=%fused_computation.8 | custom fusion | bytes 12288 | tf_op jit(solution)/shard_map/gather | solution.py:145
  51.1 3.7 fusion.25
  55.0 1.7 broadcast_multiply_fusion
  57.2 1.3 collective-permute-start.3
  58.5 3.0 collective-permute-start.2
  62.6 1.3 collective-permute-start.5
  63.9 3.0 collective-permute-start.4
  68.0 1.3 collective-permute-start.7
  69.3 3.0 collective-permute-start.6
  72.4 6.2 %gather_fusion = f32[1024]{0:T(1024)S(1)} fusion(f32[2048]{0:T(1024)S(1)} %copy-done, s32[1024]{0:T(1024)S(1)} %get-tuple-element.29), kind=kCustom, calls=%fused_computation.2 | custom fusion | bytes 12288 | tf_op jit(solution)/shard_map/gather | solution.py:156
  78.6 6.2 %gather_fusion.5 = f32[1024]{0:T(1024)S(1)} fusion(f32[2048]{0:T(1024)S(1)} %copy-done, s32[1024]{0:T(1024)S(1)} %get-tuple-element.28), kind=kCustom, calls=%fused_computation.7 | custom fusion | bytes 12288 | tf_op jit(solution)/shard_map/gather | solution.py:156
  84.7 6.2 %gather_fusion.4 = f32[1024]{0:T(1024)S(1)} fusion(f32[2048]{0:T(1024)S(1)} %copy-done.1, s32[1024]{0:T(1024)S(1)} %get-tuple-element.29), kind=kCustom, calls=%fused_computation.6 | custom fusion | bytes 12288 | tf_op jit(solution)/shard_map/gather | solution.py:156
  90.9 6.2 %gather_fusion.9 = f32[1024]{0:T(1024)S(1)} fusion(f32[2048]{0:T(1024)S(1)} %copy-done.1, s32[1024]{0:T(1024)S(1)} %get-tuple-element.28), kind=kCustom, calls=%fused_computation.11 | custom fusion | bytes 12288 | tf_op jit(solution)/shard_map/gather | solution.py:156
  98.0 8.3 %all-to-all-start = ((f32[1,5,16,256]{3,1,0,2:T(8,128)}), f32[1,5,16,256]{3,1,0,2:T(8,128)S(1)}, u32[]{:S(2)}, u32[]{:S(2)}) async-start(f32[1,5,16,256]{3,1,0,2:T(8,128)} %fusion.48), calls=%async_computation | async-start | bytes 262144 | tf_op jit(solution)/shard_map/all_to_all | solution.py:140
  106.4 7.7 %all-to-all-done = f32[1,5,16,256]{3,1,0,2:T(8,128)S(1)} async-done(((f32[1,5,16,256]{3,1,0,2:T(8,128)}), f32[1,5,16,256]{3,1,0,2:T(8,128)S(1)}, u32[]{:S(2)}, u32[]{:S(2)}) %all-to-all-start) | async-done | bytes 81952 | tf_op jit(solution)/shard_map/all_to_all | solution.py:140
  114.4 4.0 gather_fusion.10
  118.4 1.2 copy.39
  120.6 114.6 %all-reduce.7.cloned.1.call-done = f32[16,1024]{1,0:T(8,128)} async-done(((f32[16,1024]{1,0:T(8,128)}), f32[16,1024]{1,0:T(8,128)}) %all-reduce.7.cloned.1.call-update) | async-done | bytes 65552 | tf_op jit(solution)/shard_map/psum | solution.py:155
  236.0 0.9 multiply_reduce_fusion.1
  237.0 1.3 fusion.9
  238.2 1.2 fusion.115
  239.4 1.2 fusion.8
  240.7 1.2 convolution_add_fusion.5
  241.9 1.2 fusion.7
  243.2 1.2 convolution_add_fusion.4
  244.4 1.2 fusion.6
  245.6 1.2 fusion.152
  247.1 4.2 %gather_fusion.11 = f32[1024,16]{1,0:T(8,128)} fusion(f32[16,1280]{0,1:T(8,128)S(1)} %copy.44, s32[1024]{0:T(1024)S(1)} %broadcast_clamp_fusion), kind=kCustom, calls=%fused_computation.1.clone | custom fusion | bytes 135168 | tf_op jit(solution)/shard_map/jit(_take)/gather | solution.py:154
  251.3 2.2 bitcast_multiply_fusion
  253.5 128.8 %all-reduce.9.cloned.1.call-done = f32[16,1024]{0,1:T(8,128)} async-done(((f32[16,1024]{0,1:T(8,128)}), f32[16,1024]{0,1:T(8,128)}) %all-reduce.9.cloned.1.call-update) | async-done | bytes 65552 | tf_op jit(solution)/shard_map/psum | solution.py:155
  382.3 1.2 reduce_sum.57
  383.5 1.4 multiply_reduce_fusion
  384.9 1.3 fusion
  386.2 1.2 fusion.1
  387.5 1.2 fusion.2
  388.8 1.2 fusion.3
  390.4 1.2 fusion.42
  391.7 1.3 convolution_add_fusion.2
  392.9 1.3 convolution_add_fusion.1
  394.2 1.3 fusion.4
  (86 shorter events, 9.5 us)
Async XLA Ops:
  6.5 65.8 %copy-start = (f32[2048]{0:T(1024)S(1)}, f32[2048]{0:T(1024)}, u32[]{:S(2)}) copy-start(f32[2048]{0:T(1024)} %param.15) | copy-start | bytes 24580
  7.5 49.4 %collective-permute-start.1 = (f32[1,5,1,256]{3,1,0,2:T(8,128)S(1)}, f32[1,5,1,256]{3,1,0,2:T(8,128)S(1)}, u32[]{:S(2)}, u32[]{:S(2)}) collective-permute-start(f32[1,5,1,256]{3,1,0,2:T(8,128)S(1)} %get-tuple-element.21), channel_id=1, source_target_pairs={{1,0},{3,2},{5,4},{7,6},{9,8},{11,10},{13,12},{15,14},{17,16},{19,... | collective-permute-start | bytes 15368 | tf_op jit(solution)/shard_map/ppermute | solution.py:20
  8.8 48.1 %collective-permute-start = (f32[1,5,1,256]{3,1,0,2:T(8,128)S(1)}, f32[1,5,1,256]{3,1,0,2:T(8,128)S(1)}, u32[]{:S(2)}, u32[]{:S(2)}) collective-permute-start(f32[1,5,1,256]{3,1,0,2:T(8,128)S(1)} %get-tuple-element.20), channel_id=1, source_target_pairs={{0,1},{2,3},{4,5},{6,7},{8,9},{10,11},{12,13},{14,15},{16,17},{18,... | collective-permute-start | bytes 15368 | tf_op jit(solution)/shard_map/ppermute | solution.py:19
  44.1 6.2 %copy-start.9 = (f32[2,16,256]{2,1,0:T(8,128)S(1)}, f32[2,16,256]{2,1,0:T(8,128)}, u32[]{:S(2)}) copy-start(f32[2,16,256]{2,1,0:T(8,128)} %param.11) | copy-start | bytes 98308
  44.1 6.3 %copy-start.8 = (s32[5,5]{1,0:T(8,128)S(1)}, s32[5,5]{1,0:T(8,128)}, u32[]{:S(2)}) copy-start(s32[5,5]{1,0:T(8,128)} %param.17) | copy-start | bytes 304
  55.0 2.0 copy-start.10
  57.2 4.5 %collective-permute-start.3 = (f32[1,5,1,256]{3,1,0,2:T(8,128)S(1)}, f32[1,5,1,256]{3,1,0,2:T(8,128)S(1)}, u32[]{:S(2)}, u32[]{:S(2)}) collective-permute-start(f32[1,5,1,256]{3,1,0,2:T(8,128)S(1)} %get-tuple-element.19), channel_id=1, source_target_pairs={{1,0},{3,2},{5,4},{7,6},{9,8},{11,10},{13,12},{15,14},{17,16},{19,... | collective-permute-start | bytes 15368 | tf_op jit(solution)/shard_map/ppermute | solution.py:20
  58.5 3.8 collective-permute-start.2
  62.6 4.5 %collective-permute-start.5 = (f32[1,5,1,256]{3,1,0,2:T(8,128)S(1)}, f32[1,5,1,256]{3,1,0,2:T(8,128)S(1)}, u32[]{:S(2)}, u32[]{:S(2)}) collective-permute-start(f32[1,5,1,256]{3,1,0,2:T(8,128)S(1)} %get-tuple-element.17), channel_id=1, source_target_pairs={{1,0},{3,2},{5,4},{7,6},{9,8},{11,10},{13,12},{15,14},{17,16},{19,... | collective-permute-start | bytes 15368 | tf_op jit(solution)/shard_map/ppermute | solution.py:20
  63.9 3.8 collective-permute-start.4
  68.0 29.0 %collective-permute-start.7 = (f32[1,5,1,256]{3,1,0,2:T(8,128)S(1)}, f32[1,5,1,256]{3,1,0,2:T(8,128)S(1)}, u32[]{:S(2)}, u32[]{:S(2)}) collective-permute-start(f32[1,5,1,256]{3,1,0,2:T(8,128)S(1)} %get-tuple-element.15), channel_id=1, source_target_pairs={{1,0},{3,2},{5,4},{7,6},{9,8},{11,10},{13,12},{15,14},{17,16},{19,... | collective-permute-start | bytes 15368 | tf_op jit(solution)/shard_map/ppermute | solution.py:20
  69.3 27.7 %collective-permute-start.6 = (f32[1,5,1,256]{3,1,0,2:T(8,128)S(1)}, f32[1,5,1,256]{3,1,0,2:T(8,128)S(1)}, u32[]{:S(2)}, u32[]{:S(2)}) collective-permute-start(f32[1,5,1,256]{3,1,0,2:T(8,128)S(1)} %get-tuple-element.14), channel_id=1, source_target_pairs={{0,1},{2,3},{4,5},{6,7},{8,9},{10,11},{12,13},{14,15},{16,17},{18,... | collective-permute-start | bytes 15368 | tf_op jit(solution)/shard_map/ppermute | solution.py:19
  78.6 6.2 %copy-start.1 = (f32[2048]{0:T(1024)S(1)}, f32[2048]{0:T(1024)}, u32[]{:S(2)}) copy-start(f32[2048]{0:T(1024)} %param.16) | copy-start | bytes 24580
  98.0 16.1 %all-to-all-start = ((f32[1,5,16,256]{3,1,0,2:T(8,128)}), f32[1,5,16,256]{3,1,0,2:T(8,128)S(1)}, u32[]{:S(2)}, u32[]{:S(2)}) async-start(f32[1,5,16,256]{3,1,0,2:T(8,128)} %fusion.48), calls=%async_computation | async-start | bytes 262144 | tf_op jit(solution)/shard_map/all_to_all | solution.py:140
  106.3 128.8 %all-reduce.7.cloned.1.call-start = ((), (), s32[]{:S(2)}) async-start(), calls=%async_computation.1 | async-start | bytes 131072 | tf_op jit(solution)/shard_map/psum | solution.py:155
  118.4 118.5 %copy-start.7 = (f32[256,256]{1,0:T(8,128)S(1)}, f32[256,256]{1,0:T(8,128)}, u32[]{:S(2)}) copy-start(f32[256,256]{1,0:T(8,128)} %get-tuple-element.68) | copy-start | bytes 786436
  120.3 261.9 %all-reduce.9.cloned.1.call-start = ((), (), s32[]{:S(2)}) async-start(), calls=%async_computation.2 | async-start | bytes 1048576 | tf_op jit(solution)/shard_map/psum | solution.py:155
  236.9 2.5 copy-start.6
  239.4 2.5 copy-start.5
  241.9 2.5 copy-start.4
  386.2 1.3 copy-start.3
  387.5 1.3 copy-start.2
Sparse Core Ops, SparseCore 0:
  120.5 114.6 all-reduce.6
  253.6 128.6 all-reduce.8
where the time goes:
time: 404 us; the launch traced here: 403 us
  waiting for transfers between devices  253 us (63%)
  local copies, waits for them, and re-layouts  73.4 us (18%)
  starting transfers between devices  25.9 us (6%)
  matrix products  20.7 us (5%)
  other arithmetic  16.5 us (4%)
  between operations  14.1 us (3%)
    psum x2, waiting for transfers between devices, per_device(): priors = lax.psum(partial_priors, ('mem', 'row'))  243 us
    gather x4, local copies, waits for them, and re-layouts, per_device(): anomaly, adjust = innovations(priors, obs_value[picked], obs_var[picked])  24.6 us
    gather x2, local copies, waits for them, and re-layouts, per_device(): obs_field = field_all[picked]  12.3 us
    gather x2, local copies, waits for them, and re-layouts, per_device(): obs_row = row_all[picked]  12.3 us
    gather x2, local copies, waits for them, and re-layouts, per_device(): obs_col = col_all[picked]  12.3 us
    ppermute x4, starting transfers between devices, extended(): before = lax.ppermute(last, axis, up)  12.1 us
    dot_general x8, matrix products, regress(): lax.dot_general(centred, anomaly[:, offset:offset + obs_block], (((0,), (...  9.99 us
    dot_general x8, matrix products, regress(): lax.dot_general(adjust[:, offset:offset + obs_block], weights.reshape(n_c...  9.76 us
  transfers between devices with their start and end apart: 11, of which 5 were waited for; matrix products, arithmetic and copies ran while one was open for 17% of the time, Pallas kernels for 0%

commit v1 on v0

--- a/solution.py
+++ b/solution.py
@@ -152,7 +152,7 @@
             + obs_col
         )
         partial_priors = jnp.take(ensemble_now, local_ids, axis=1) * owned[None, :]
-        priors = lax.psum(partial_priors, ("mem", "row"))
+        priors = lax.psum(lax.psum(partial_priors, "row"), "mem")
         anomaly, adjust = innovations(priors, obs_value[picked], obs_var[picked])
         ensemble_now = regress(
             ensemble_now, base_row, obs_field, obs_row, obs_col, anomaly, adjust, field_mask, n_cols

time: 404 us -> 407 us (level)
    psum x2 -> x4, waiting for transfers between devices: 243 us -> 241 us  [per_device(): priors = lax.psum(lax.psum(partial_priors, 'row'), 'mem')]
  transfers between devices with their start and end apart: 11 -> 13, of which waited for: 5 -> 7; matrix products, arithmetic and copies ran while one was open for 17% -> 18% of each run, Pallas kernels for 0% -> 0%
where the time goes in v1:
time: 407 us; the launch traced here: 406 us
  waiting for transfers between devices  251 us (62%)
  local copies, waits for them, and re-layouts  73.2 us (18%)
  starting transfers between devices  26.2 us (6%)
  matrix products  24.1 us (6%)
  other arithmetic  17.9 us (4%)
  between operations  13.8 us (3%)
    psum x4, waiting for transfers between devices, per_device(): priors = lax.psum(lax.psum(partial_priors, 'row'), 'mem')  241 us
    gather x4, local copies, waits for them, and re-layouts, per_device(): anomaly, adjust = innovations(priors, obs_value[picked], obs_var[picked])  24.6 us
    gather x2, local copies, waits for them, and re-layouts, per_device(): obs_field = field_all[picked]  12.3 us
    gather x2, local copies, waits for them, and re-layouts, per_device(): obs_row = row_all[picked]  12.3 us
    gather x2, local copies, waits for them, and re-layouts, per_device(): obs_col = col_all[picked]  12.3 us
    ppermute x4, starting transfers between devices, extended(): before = lax.ppermute(last, axis, up)  12.1 us
    dot_general x8, matrix products, regress(): lax.dot_general(centred, anomaly[:, offset:offset + obs_block], (((0,), (...  11 us
    dot_general x8, matrix products, regress(): lax.dot_general(adjust[:, offset:offset + obs_block], weights.reshape(n_c...  9.76 us
  transfers between devices with their start and end apart: 13, of which 7 were waited for; matrix products, arithmetic and copies ran while one was open for 18% of the time, Pallas kernels for 0%

profile of v1, /device:TPU:0, one launch (start us, length us, event | category | flops | bytes accessed | tf_op | source)
XLA Modules:
  0.0 405.8 jit_solution(16601850915948569768)
XLA Ops:
  7.5 1.3 collective-permute-start.1
  8.8 3.0 collective-permute-start
  13.3 6.1 %gather_fusion.8 = s32[1024]{0:T(1024)S(1)} fusion(s32[2048]{0:T(1024)S(1)} %get-tuple-element.33, s32[1024]{0:T(1024)S(1)} %get-tuple-element.28), kind=kCustom, calls=%fused_computation.10 | custom fusion | bytes 12288 | tf_op jit(solution)/shard_map/gather | solution.py:147
  19.4 6.2 %gather_fusion.7 = s32[1024]{0:T(1024)S(1)} fusion(s32[2048]{0:T(1024)S(1)} %get-tuple-element.32, s32[1024]{0:T(1024)S(1)} %get-tuple-element.28), kind=kCustom, calls=%fused_computation.9 | custom fusion | bytes 12288 | tf_op jit(solution)/shard_map/gather | solution.py:146
  25.6 6.2 %gather_fusion.3 = s32[1024]{0:T(1024)S(1)} fusion(s32[2048]{0:T(1024)S(1)} %get-tuple-element.33, s32[1024]{0:T(1024)S(1)} %get-tuple-element.29), kind=kCustom, calls=%fused_computation.5 | custom fusion | bytes 12288 | tf_op jit(solution)/shard_map/gather | solution.py:147
  31.8 6.2 %gather_fusion.2 = s32[1024]{0:T(1024)S(1)} fusion(s32[2048]{0:T(1024)S(1)} %get-tuple-element.32, s32[1024]{0:T(1024)S(1)} %get-tuple-element.29), kind=kCustom, calls=%fused_computation.4 | custom fusion | bytes 12288 | tf_op jit(solution)/shard_map/gather | solution.py:146
  37.9 6.2 %gather_fusion.1 = s32[1024]{0:T(1024)S(1)} fusion(s32[2048]{0:T(1024)S(1)} %get-tuple-element.34, s32[1024]{0:T(1024)S(1)} %get-tuple-element.29), kind=kCustom, calls=%fused_computation.3 | custom fusion | bytes 12288 | tf_op jit(solution)/shard_map/gather | solution.py:145
  44.1 6.2 %gather_fusion.6 = s32[1024]{0:T(1024)S(1)} fusion(s32[2048]{0:T(1024)S(1)} %get-tuple-element.34, s32[1024]{0:T(1024)S(1)} %get-tuple-element.28), kind=kCustom, calls=%fused_computation.8 | custom fusion | bytes 12288 | tf_op jit(solution)/shard_map/gather | solution.py:145
  53.4 3.8 fusion.25
  58.5 1.3 collective-permute-start.3
  59.8 3.0 collective-permute-start.2
  63.9 1.3 collective-permute-start.5
  65.2 3.0 collective-permute-start.4
  69.3 1.3 collective-permute-start.7
  70.6 3.0 collective-permute-start.6
  73.7 6.2 %gather_fusion = f32[1024]{0:T(1024)S(1)} fusion(f32[2048]{0:T(1024)S(1)} %copy-done, s32[1024]{0:T(1024)S(1)} %get-tuple-element.29), kind=kCustom, calls=%fused_computation.2 | custom fusion | bytes 12288 | tf_op jit(solution)/shard_map/gather | solution.py:156
  79.9 6.2 %gather_fusion.4 = f32[1024]{0:T(1024)S(1)} fusion(f32[2048]{0:T(1024)S(1)} %copy-done.1, s32[1024]{0:T(1024)S(1)} %get-tuple-element.29), kind=kCustom, calls=%fused_computation.6 | custom fusion | bytes 12288 | tf_op jit(solution)/shard_map/gather | solution.py:156
  87.0 8.3 %all-to-all-start = ((f32[1,5,16,256]{3,1,0,2:T(8,128)}), f32[1,5,16,256]{3,1,0,2:T(8,128)S(1)}, u32[]{:S(2)}, u32[]{:S(2)}) async-start(f32[1,5,16,256]{3,1,0,2:T(8,128)} %fusion.48), calls=%async_computation | async-start | bytes 262144 | tf_op jit(solution)/shard_map/all_to_all | solution.py:140
  95.4 7.7 %all-to-all-done = f32[1,5,16,256]{3,1,0,2:T(8,128)S(1)} async-done(((f32[1,5,16,256]{3,1,0,2:T(8,128)}), f32[1,5,16,256]{3,1,0,2:T(8,128)S(1)}, u32[]{:S(2)}, u32[]{:S(2)}) %all-to-all-start) | async-done | bytes 81952 | tf_op jit(solution)/shard_map/all_to_all | solution.py:140
  103.4 4.0 gather_fusion.10
  107.4 1.2 copy.39
  108.6 1.3 bitcast_multiply_fusion.1
  110.0 15.0 %all-reduce.9.cloned.1.call-done = f32[16,1024]{1,0:T(8,128)} async-done(((f32[16,1024]{1,0:T(8,128)}), f32[16,1024]{1,0:T(8,128)}) %all-reduce.9.cloned.1.call-update) | async-done | bytes 65552 | tf_op jit(solution)/shard_map/psum | solution.py:155
  125.3 108.4 %all-reduce.11.cloned.1.call-done = f32[16,1024]{1,0:T(8,128)} async-done(((f32[16,1024]{1,0:T(8,128)}), f32[16,1024]{1,0:T(8,128)}) %all-reduce.11.cloned.1.call-update) | async-done | bytes 65552 | tf_op jit(solution)/shard_map/psum | solution.py:155
  235.4 2.2 fusion.9
  238.9 1.3 fusion.8
  240.2 1.2 convolution_add_fusion.5
  241.4 1.2 fusion.7
  242.7 1.2 convolution_add_fusion.4
  243.9 1.3 fusion.6
  245.1 1.2 fusion.152
  246.6 4.0 gather_fusion.11
  250.6 2.2 bitcast_multiply_fusion
  253.2 1.8 broadcast_multiply_fusion
  255.0 6.1 %gather_fusion.5 = f32[1024]{0:T(1024)S(1)} fusion(f32[2048]{0:T(1024)S(1)} %copy-done, s32[1024]{0:T(1024)S(1)} %get-tuple-element.28), kind=kCustom, calls=%fused_computation.7 | custom fusion | bytes 12288 | tf_op jit(solution)/shard_map/gather | solution.py:156
  261.1 6.2 %gather_fusion.9 = f32[1024]{0:T(1024)S(1)} fusion(f32[2048]{0:T(1024)S(1)} %copy-done.1, s32[1024]{0:T(1024)S(1)} %get-tuple-element.28), kind=kCustom, calls=%fused_computation.11 | custom fusion | bytes 12288 | tf_op jit(solution)/shard_map/gather | solution.py:156
  267.3 3.6 all-reduce.13.cloned.1.call-done
  270.9 114.5 %all-reduce.15.cloned.1.call-done = f32[16,1024]{0,1:T(8,128)} async-done(((f32[16,1024]{0,1:T(8,128)}), f32[16,1024]{0,1:T(8,128)}) %all-reduce.15.cloned.1.call-update) | async-done | bytes 65552 | tf_op jit(solution)/shard_map/psum | solution.py:155
  385.4 1.2 reduce_sum.57
  386.6 1.4 multiply_reduce_fusion
  388.0 1.3 fusion
  389.3 1.2 fusion.1
  390.6 1.2 fusion.2
  391.9 1.2 fusion.3
  393.6 1.2 fusion.42
  394.8 1.3 convolution_add_fusion.2
  396.1 1.3 convolution_add_fusion.1
  397.3 1.3 fusion.4
  (102 shorter events, 15.1 us)
Async XLA Ops:
  6.5 67.1 %copy-start = (f32[2048]{0:T(1024)S(1)}, f32[2048]{0:T(1024)}, u32[]{:S(2)}) copy-start(f32[2048]{0:T(1024)} %param.15) | copy-start | bytes 24580
  7.5 50.7 %collective-permute-start.1 = (f32[1,5,1,256]{3,1,0,2:T(8,128)S(1)}, f32[1,5,1,256]{3,1,0,2:T(8,128)S(1)}, u32[]{:S(2)}, u32[]{:S(2)}) collective-permute-start(f32[1,5,1,256]{3,1,0,2:T(8,128)S(1)} %get-tuple-element.21), channel_id=1, source_target_pairs={{1,0},{3,2},{5,4},{7,6},{9,8},{11,10},{13,12},{15,14},{17,16},{19,... | collective-permute-start | bytes 15368 | tf_op jit(solution)/shard_map/ppermute | solution.py:20
  8.8 49.4 %collective-permute-start = (f32[1,5,1,256]{3,1,0,2:T(8,128)S(1)}, f32[1,5,1,256]{3,1,0,2:T(8,128)S(1)}, u32[]{:S(2)}, u32[]{:S(2)}) collective-permute-start(f32[1,5,1,256]{3,1,0,2:T(8,128)S(1)} %get-tuple-element.20), channel_id=1, source_target_pairs={{0,1},{2,3},{4,5},{6,7},{8,9},{10,11},{12,13},{14,15},{16,17},{18,... | collective-permute-start | bytes 15368 | tf_op jit(solution)/shard_map/ppermute | solution.py:19
  44.1 6.2 %copy-start.10 = (f32[2,16,256]{2,1,0:T(8,128)S(1)}, f32[2,16,256]{2,1,0:T(8,128)}, u32[]{:S(2)}) copy-start(f32[2,16,256]{2,1,0:T(8,128)} %param.11) | copy-start | bytes 98308
  44.1 6.9 %copy-start.9 = (s32[5,5]{1,0:T(8,128)S(1)}, s32[5,5]{1,0:T(8,128)}, u32[]{:S(2)}) copy-start(s32[5,5]{1,0:T(8,128)} %param.17) | copy-start | bytes 304
  57.2 1.1 copy-start.15
  58.5 4.5 %collective-permute-start.3 = (f32[1,5,1,256]{3,1,0,2:T(8,128)S(1)}, f32[1,5,1,256]{3,1,0,2:T(8,128)S(1)}, u32[]{:S(2)}, u32[]{:S(2)}) collective-permute-start(f32[1,5,1,256]{3,1,0,2:T(8,128)S(1)} %get-tuple-element.19), channel_id=1, source_target_pairs={{1,0},{3,2},{5,4},{7,6},{9,8},{11,10},{13,12},{15,14},{17,16},{19,... | collective-permute-start | bytes 15368 | tf_op jit(solution)/shard_map/ppermute | solution.py:20
  59.8 3.8 collective-permute-start.2
  63.9 4.5 %collective-permute-start.5 = (f32[1,5,1,256]{3,1,0,2:T(8,128)S(1)}, f32[1,5,1,256]{3,1,0,2:T(8,128)S(1)}, u32[]{:S(2)}, u32[]{:S(2)}) collective-permute-start(f32[1,5,1,256]{3,1,0,2:T(8,128)S(1)} %get-tuple-element.17), channel_id=1, source_target_pairs={{1,0},{3,2},{5,4},{7,6},{9,8},{11,10},{13,12},{15,14},{17,16},{19,... | collective-permute-start | bytes 15368 | tf_op jit(solution)/shard_map/ppermute | solution.py:20
  65.2 3.8 collective-permute-start.4
  69.3 16.7 %collective-permute-start.7 = (f32[1,5,1,256]{3,1,0,2:T(8,128)S(1)}, f32[1,5,1,256]{3,1,0,2:T(8,128)S(1)}, u32[]{:S(2)}, u32[]{:S(2)}) collective-permute-start(f32[1,5,1,256]{3,1,0,2:T(8,128)S(1)} %get-tuple-element.15), channel_id=1, source_target_pairs={{1,0},{3,2},{5,4},{7,6},{9,8},{11,10},{13,12},{15,14},{17,16},{19,... | collective-permute-start | bytes 15368 | tf_op jit(solution)/shard_map/ppermute | solution.py:20
  70.6 15.4 %collective-permute-start.6 = (f32[1,5,1,256]{3,1,0,2:T(8,128)S(1)}, f32[1,5,1,256]{3,1,0,2:T(8,128)S(1)}, u32[]{:S(2)}, u32[]{:S(2)}) collective-permute-start(f32[1,5,1,256]{3,1,0,2:T(8,128)S(1)} %get-tuple-element.14), channel_id=1, source_target_pairs={{0,1},{2,3},{4,5},{6,7},{8,9},{10,11},{12,13},{14,15},{16,17},{18,... | collective-permute-start | bytes 15368 | tf_op jit(solution)/shard_map/ppermute | solution.py:19
  73.7 6.2 %copy-start.1 = (f32[2048]{0:T(1024)S(1)}, f32[2048]{0:T(1024)}, u32[]{:S(2)}) copy-start(f32[2048]{0:T(1024)} %param.16) | copy-start | bytes 24580
  87.0 16.1 %all-to-all-start = ((f32[1,5,16,256]{3,1,0,2:T(8,128)}), f32[1,5,16,256]{3,1,0,2:T(8,128)S(1)}, u32[]{:S(2)}, u32[]{:S(2)}) async-start(f32[1,5,16,256]{3,1,0,2:T(8,128)} %fusion.48), calls=%async_computation | async-start | bytes 262144 | tf_op jit(solution)/shard_map/all_to_all | solution.py:140
  95.3 29.7 %all-reduce.9.cloned.1.call-start = ((), (), s32[]{:S(2)}) async-start(), calls=%async_computation.1 | async-start | bytes 131072 | tf_op jit(solution)/shard_map/psum | solution.py:155
  107.4 128.0 %copy-start.13 = (f32[5,256]{1,0:T(8,128)S(1)}, f32[5,256]{1,0:T(8,128)}, u32[]{:S(2)}) copy-start(f32[5,256]{1,0:T(8,128)} %convolution_bitcast_fusion.7) | copy-start | bytes 15364
  109.9 123.7 %all-reduce.11.cloned.1.call-start = ((), (), s32[]{:S(2)}) async-start(), calls=%async_computation.2 | async-start | bytes 131072 | tf_op jit(solution)/shard_map/psum | solution.py:155
  125.0 145.8 %all-reduce.13.cloned.1.call-start = ((), (), s32[]{:S(2)}) async-start(), calls=%async_computation.3 | async-start | bytes 1048576 | tf_op jit(solution)/shard_map/psum | solution.py:155
  235.4 3.5 copy-start.8
  235.4 3.5 copy-start.12
  238.9 2.5 copy-start.7
  238.9 2.5 copy-start.11
  241.4 2.5 copy-start.6
  241.4 2.5 copy-start.14
  250.6 2.6 copy-start.4
  250.6 2.6 copy-start.5
  252.9 132.5 %all-reduce.15.cloned.1.call-start = ((), (), s32[]{:S(2)}) async-start(), calls=%async_computation.4 | async-start | bytes 1048576 | tf_op jit(solution)/shard_map/psum | solution.py:155
  389.3 1.3 copy-start.3
  390.6 1.3 copy-start.2
Sparse Core Ops, SparseCore 0:
  110.1 14.8 all-reduce.8
  130.5 103.1 all-reduce.10
  253.0 17.7 all-reduce.12
  275.8 109.4 all-reduce.14
